TPU v7x, 256 devices: a whole 4x4x8 slice. The times are simulated.
256 devices in a mesh: dp: 16 (over y_lo, z), fsdp: 16 (over x, y_hi, core).
Axes of the slice: x: 4, y: 4 (y_hi: 2, y_lo: 2; y = y_hi * 2 + y_lo), z: 8, core: 2. Of those that a mesh axis runs over, the one named last changes fastest.
Arguments:
- frames: bfloat16 [256, 256, 1536], P(('dp', 'fsdp')), may hold values from -6 to 6
- cotangent: bfloat16 [256, 256, 1536], P(('dp', 'fsdp')), may hold values from -6 to 6
- lengths: int32 [256], P(('dp', 'fsdp')), may hold values from 64 to 256, as said below
- weight_slots: bfloat16 [2304, 3072], P('fsdp'), may hold values from -0.15625 to 0.15625
- owner_rows: int32 [2304], replicated, may hold values from -1 to 1535, as said below
- gain_in: float32 [1536], replicated, may hold values from 0.5 to 1.5
- gain_mid: float32 [1536], replicated, may hold values from 0.5 to 1.5
- kernel: float32 [32, 1536], replicated, may hold values from -1 to 1
Outputs:
- frame_grads: bfloat16 [256, 256, 1536], P(('dp', 'fsdp'))
- weight_grads: bfloat16 [2304, 3072], P('fsdp')
- gain_in_grad: float32 [1536], replicated
- gain_mid_grad: float32 [1536], replicated
- kernel_grad: float32 [32, 1536], replicated
Inputs may be any that keep to these rules, and one draw needn't show every extreme that they name: `owner_rows`: slots o * 144 to o * 144 + 143 belong to owner o (index o of fsdp): first the rows it holds, then -1. Each of the 1536 rows is named by exactly one slot. An owner holds between 48 and 144 rows, and some owner holds exactly 144. Rows of weight_slots in slots marked -1 are not used. `lengths`: some utterance has all 256 frames in use.
All inputs are finite; a program needn't handle non-finite values.
Results may differ from a plain program's by a relative error of at most 0.02.
Values may be sent and summed in bfloat16 or wider, within the bound.
A program may use at most 192 MiB of HBM per device.

v0:
```python
import functools
import jax
import jax.numpy as jnp
from jax import lax
from jax.experimental import pallas as pl
from jax.experimental.pallas import tpu as pltpu
from jax.sharding import PartitionSpec as P

MESH = pl.DeviceIdType.MESH
NX, NY, NZ = 4, 4, 8
PIECES = 3
PARTS = 3
BLOCK = 72
LANES = 128
SMALL = 32
EPSILON = 1e-05
STEP = 32
SEG = 8
WIDE = 256
PART_AXES = ("zxy", "xyz", "yxz")


def place():
    d = lax.axis_index("dp")
    f = lax.axis_index("fsdp")
    return f // 4, (f // 2) % 2, d // NZ, d % NZ, f % 2


def device(x, yh, yl, z, c):
    return (yl * NZ + z, (x * 2 + yh) * 2 + c)


def wide(value):
    return value.astype(jnp.float32)


def split_index(i, lead):
    index = []
    for size in reversed(lead):
        index.append(i % size)
        i = i // size
    return tuple(reversed(index))


def add_into(dst, sources, lead):
    total = 1
    for size in lead:
        total *= size

    def one(i, carry):
        index = split_index(i, lead)
        value = wide(dst[index])
        for src in sources:
            value = value + wide(src[index])
        dst[index] = value.astype(dst.dtype)
        return carry

    if total == 1:
        one(0, 0)
    else:
        lax.fori_loop(0, total, one, 0)


def contract_last(a, b):
    return lax.dot_general(a, b, (((1,), (1,)), ((), ())), preferred_element_type=jnp.float32)


def over_lanes(value, count):
    return jnp.sum(value, axis=-1, keepdims=True) * (1.0 / count)


def extend(ext, value, taps):
    before = taps // 2
    seg = lax.broadcasted_iota(jnp.int32, (before, SEG, LANES), 1)
    ext[pl.ds(before, STEP)] = value
    late = pltpu.roll(value[STEP - before :], 1, 1)
    ext[pl.ds(0, before)] = jnp.where(seg == 0, 0.0, late)
    early = pltpu.roll(value[:before], SEG - 1, 1)
    ext[pl.ds(before + STEP, before)] = jnp.where(seg == SEG - 1, 0.0, early)


def module_kernel(
    length_ref, frames_ref, cot_ref, w_ref, owner_ref, gain_in_ref, gain_mid_ref, taps_ref,
    out_ref, rows_ref, small_out,
    weight, natural, cots, normed, in_slots, slots_t, grad, means, inverses, left, gate, held,
    conv, deriv, ext_d, taps_wide, keep, acc_a, acc_b, back, small, small_split,
    theirs_t, theirs_g, sums, low, near_x, near_y, near_z, mid_0, mid_1, mid_2, far_0, far_1, far_2,
    small_sum, small_sib, small_z, small_x, small_y, finals, other_finals,
    keep_sem, w_send, w_recv, swap_send, swap_recv, send, recv, direct_send, direct_recv, small_send, small_recv,
    out_send, out_recv, sib_send, sib_recv,
):
    x, yh, yl, z, c = place()
    y = yh * 2 + yl
    f32 = jnp.float32
    features = frames_ref.shape[1]
    slabs = features // LANES
    taps = taps_ref.shape[0]
    slots = owner_ref.shape[1]
    blocks = features // WIDE
    tokens = STEP * SEG
    cap, width = w_ref.shape
    part_cols = features // PARTS

    def at_x(i):
        return device(i % NX, yh, yl, z, c)

    def at_y(i):
        return device(x, (i % NY) // 2, i % 2, z, c)

    def at_z(i):
        return device(x, yh, yl, i % NZ, c)

    sib = device(x, yh, yl, z, 1 - c)
    to_ac = device(x, 1 - yh, 1 - yl, z, c)
    to_ys = device(x, yh, 1 - yl, z, c)
    pending = []

    def push(src, dst, send_sem, recv_sem, to):
        copy = pltpu.make_async_remote_copy(
            src_ref=src, dst_ref=dst, send_sem=send_sem, recv_sem=recv_sem,
            device_id=to, device_id_type=MESH,
        )
        copy.start()
        pending.append(copy)
        return copy

    def landed(ref, send_sem, recv_sem):
        pltpu.make_async_remote_copy(
            src_ref=ref, dst_ref=ref, send_sem=send_sem, recv_sem=recv_sem,
            device_id=sib, device_id_type=MESH,
        ).wait_recv()

    peers = (
        [sib]
        + [at_x(x + i) for i in range(1, NX)]
        + [at_y(y + i) for i in range(1, NY)]
        + [at_z(z + i) for i in range(1, NZ)]
    )
    barrier = pltpu.get_barrier_semaphore()
    for peer in peers:
        pl.semaphore_signal(barrier, inc=1, device_id=peer, device_id_type=MESH)
    pl.semaphore_wait(barrier, len(peers))

    xs = [x, (x + 3) % NX, (x + 1) % NX, (x + 2) % NX]
    to_xp, to_xm, to_zp, to_zm = at_x(x + 1), at_x(x + 3), at_z(z + 1), at_z(z + NZ - 1)
    third = width // 3
    piece_rows = cap // PIECES
    par = z % 2
    base = par * third

    def cols(start, size):
        return pl.ds(pl.multiple_of(start, third // 2), size)

    window = cols(base, 2 * third)
    halves = [cols(base, third), cols(base + third, third)]
    mine = cols(base + yl * third, third)
    other = cols(base + (1 - yl) * third, third)
    shared = [cols(base + par * third, third // 2), cols(base + par * third + third // 2, third // 2)]
    theirs = [cols((1 - par) * 2 * third, third // 2), cols((1 - par) * 2 * third + third // 2, third // 2)]

    def owner(k, other_row):
        return (xs[k] * 2 + (1 - yh if other_row else yh)) * 2 + c

    def piece(ref, q, span):
        return ref.at[pl.ds(q * piece_rows, piece_rows), span]

    def w_push(index, q, src, dst, to):
        push(src, dst, w_send.at[index, q], w_recv.at[index, q], to)

    def pass_on(index, q, who, span, to):
        ref = piece(weight.at[who], q, span)
        w_push(index, q, ref, ref, to)

    def arrive(index, q, who, span):
        landed(piece(weight.at[who], q, span), w_send.at[index, q], w_recv.at[index, q])

    me = owner(0, False)
    x_copies = [
        [
            pltpu.make_async_remote_copy(
                src_ref=piece(w_ref, q, window), dst_ref=piece(weight.at[me], q, window),
                send_sem=w_send.at[index, q], recv_sem=w_recv.at[index, q],
                device_id=to, device_id_type=MESH,
            )
            for index, to in ((1, to_xp), (2, to_xm))
        ]
        for q in range(PIECES)
    ]

    def x_next(q):
        for copy in x_copies[q - 1]:
            copy.wait_send()
        for copy in x_copies[q]:
            copy.start()

    for copy in x_copies[0]:
        copy.start()
    pending.extend(x_copies[-1])
    for q in range(PIECES):
        w_push(3, q, piece(w_ref, q, mine), piece(weight.at[me], q, mine), to_ac)
    w_push(0, 0, w_ref, weight.at[me], sib)
    own_copy = pltpu.make_async_copy(w_ref, weight.at[me], keep_sem)
    own_copy.start()

    def z_out(slot, q, who):
        pass_on(13 + slot, q, who, shared[0], to_zp)
        pass_on(20 + slot, q, who, shared[1], to_zm)

    units = [(1, False), (2, False), (3, False), (0, True), (1, True), (2, True), (3, True)]

    def x_near(k, q):
        arrive(k, q, owner(k, False), window)
        pass_on(6 + k, q, owner(k, False), halves[k - 1], (to_xp, to_xm)[k - 1])
        pass_on(3 + k, q, owner(k, False), mine, to_ac)
        z_out(k - 1, q, owner(k, False))
        pass_on(26 + k, q, owner(k, False), window, sib)

    def x_far(q):
        arrive(7, q, owner(3, False), halves[0])
        arrive(8, q, owner(3, False), halves[1])
        pass_on(6, q, owner(3, False), mine, to_ac)
        z_out(2, q, owner(3, False))
        pass_on(29, q, owner(3, False), halves[0], sib)
        pass_on(30, q, owner(3, False), halves[1], sib)

    def across(k, q):
        arrive(3 + k, q, owner(k, True), other)
        pass_on(9 + k, q, owner(k, True), other, to_ys)
        pass_on(31 + k, q, owner(k, True), other, sib)

    def beside(k, q):
        arrive(9 + k, q, owner(k, True), mine)
        z_out(3 + k, q, owner(k, True))
        pass_on(35 + k, q, owner(k, True), mine, sib)

    def z_in(slot, q):
        who = owner(*units[slot])
        arrive(13 + slot, q, who, theirs[0])
        pass_on(39 + slot, q, who, theirs[0], sib)
        arrive(20 + slot, q, who, theirs[1])
        pass_on(46 + slot, q, who, theirs[1], sib)

    def flip(who):
        return who + 1 - 2 * c

    def from_sibling():
        landed(weight.at[flip(me)], w_send.at[0, 0], w_recv.at[0, 0])
        for q in range(PIECES):
            arrive(27, q, flip(owner(1, False)), window)
            arrive(28, q, flip(owner(2, False)), window)
            arrive(29, q, flip(owner(3, False)), halves[0])
            arrive(30, q, flip(owner(3, False)), halves[1])
            for k in range(4):
                arrive(31 + k, q, flip(owner(k, True)), other)
                arrive(35 + k, q, flip(owner(k, True)), mine)
            for slot in range(7):
                arrive(39 + slot, q, flip(owner(*units[slot])), theirs[0])
                arrive(46 + slot, q, flip(owner(*units[slot])), theirs[1])
        own_copy.wait()

    def row(ref, k, j):
        return ref[k, pl.ds(j, SEG, stride=STEP), :]

    def gain(ref, k):
        return ref[:, pl.ds(k * LANES, LANES)]

    def prepare():
        for k in range(slabs):
            lanes = pl.ds(k * LANES, LANES)
            natural[k] = wide(frames_ref[:, lanes])
            taps_wide[k] = jnp.broadcast_to(taps_ref[:, lanes][:, None, :], (taps, SEG, LANES))
        step_of = lax.broadcasted_iota(jnp.int32, (STEP, SEG, LANES), 0)
        seg_of = lax.broadcasted_iota(jnp.int32, (STEP, SEG, LANES), 1)
        keep[...] = (seg_of * STEP + step_of < length_ref[0]).astype(f32)

    def prepare_cots():
        for k in range(slabs):
            cots[k] = wide(cot_ref[:, pl.ds(k * LANES, LANES)])
        small[...] = jnp.zeros_like(small)

    def norm_pair(i, carry):
        parts = []
        for j in (2 * i, 2 * i + 1):
            values = [row(natural, k, j) for k in range(slabs)]
            total = values[0]
            for v in values[1:]:
                total = total + v
            mean = over_lanes(total, features)
            values = [v - mean for v in values]
            total = values[0] * values[0]
            for v in values[1:]:
                total = total + v * v
            inverse = lax.rsqrt(over_lanes(total, features) + EPSILON)
            means[j] = jnp.broadcast_to(mean, (SEG, LANES))
            inverses[j] = jnp.broadcast_to(inverse, (SEG, LANES))
            parts.append([v * inverse * gain(gain_in_ref, k) for k, v in enumerate(values)])
        for k in range(slabs):
            pair = jnp.concatenate([parts[0][k], parts[1][k]], axis=0)
            normed[pl.ds(pl.multiple_of(i * 16, 16), 16), pl.ds(k * LANES, LANES)] = pair.astype(normed.dtype)
        return carry

    def norm_some(i):
        lax.fori_loop(4 * i, 4 * i + 4, norm_pair, 0)

    def slab_mask(owned, k):
        return jnp.where((owned >= k * LANES) & (owned < (k + 1) * LANES), 1.0, 0.0).astype(normed.dtype)

    def choose(i):
        span = pl.ds(i * WIDE, WIDE)
        rows = lax.broadcasted_iota(jnp.int32, (LANES, WIDE), 0)
        owned = owner_ref[:, span]
        line = jnp.where(rows == owned % LANES, 1.0, 0.0).astype(normed.dtype)
        low[:, span] = line
        picked = jnp.concatenate([line * slab_mask(owned, k) for k in range(slabs)], axis=0)
        moved = jnp.dot(normed[...], picked, preferred_element_type=f32)
        in_slots[:, span] = moved.astype(in_slots.dtype)
        slots_t[span, :] = jnp.transpose(moved).astype(slots_t.dtype)

    slots_copy = pltpu.make_async_remote_copy(
        src_ref=slots_t, dst_ref=theirs_t, send_sem=swap_send.at[0], recv_sem=swap_recv.at[0],
        device_id=sib, device_id_type=MESH,
    )

    def swap_slots():
        slots_copy.start()

    part = functools.partial
    fill = [part(norm_some, i) for i in range(STEP // 8)]
    fill += [part(choose, i) for i in range(slots // WIDE)] + [swap_slots, prepare_cots]
    steps = []
    last = PIECES - 1
    for q in range(PIECES):
        if q < last:
            steps += [part(x_next, q + 1)]
        steps += [part(x_near, 1, q), part(x_near, 2, q), part(across, 0, q)]
        if q > 0:
            steps += [part(across, 1, q - 1), part(across, 2, q - 1), part(beside, 0, q - 1)]
    steps += [part(beside, 0, last)]
    steps += [part(x_far, 0), part(across, 1, last), part(across, 2, last)]
    for q in range(PIECES):
        steps += [part(beside, 1, q), part(beside, 2, q)]
        if q < last:
            steps += [part(x_far, q + 1)]
        steps += [part(across, 3, q), part(z_in, 0, q), part(z_in, 1, q), part(z_in, 3, q)]
    for q in range(PIECES):
        steps += [part(beside, 3, q), part(z_in, 2, q), part(z_in, 4, q), part(z_in, 5, q)]
    for q in range(PIECES):
        steps += [part(z_in, 6, q)]

    prepare()
    for task in fill[:2]:
        task()
    fill = fill[2:]
    for step in steps:
        step()
        if fill:
            fill.pop(0)()
    for task in fill:
        task()
    from_sibling()

    acc_a[...] = jnp.zeros_like(acc_a)

    def tap_rows(ext, k, sign, put):
        def one(b, carry):
            start = b * SEG
            first = start if sign > 0 else start + 1
            lines = [ext[first + i] for i in range(taps + SEG - 1)]
            totals = [None] * SEG
            for t in range(taps):
                w = taps_wide[k, t if sign > 0 else taps - 1 - t]
                for i in range(SEG):
                    term = w * lines[i + t]
                    totals[i] = term if totals[i] is None else totals[i] + term
            for i in range(SEG):
                put(start + i, totals[i])
            return carry

        lax.fori_loop(0, STEP // SEG, one, 0)

    def weight_cols(start):
        return weight[:, :, pl.ds(pl.multiple_of(start, WIDE), WIDE)].reshape(slots, WIDE)

    def forward(i, carry):
        value = jnp.dot(in_slots[...], weight_cols(i * WIDE), preferred_element_type=f32)
        opened = jnp.dot(in_slots[...], weight_cols(features + i * WIDE), preferred_element_type=f32)
        opened = jax.nn.sigmoid(opened)
        for h in range(WIDE // LANES):
            k = i * (WIDE // LANES) + h
            a = value[:, h * LANES : (h + 1) * LANES].reshape(STEP, SEG, LANES)
            s = opened[:, h * LANES : (h + 1) * LANES].reshape(STEP, SEG, LANES)
            left[k] = a
            gate[k] = s
            extend(held.at[k], a * s * keep[...], taps)

            def put(j, v, k=k):
                conv[k, j] = v
                acc_a[j] = acc_a[j] + v

            tap_rows(held.at[k], k, 1, put)
        return carry

    lax.fori_loop(0, blocks, forward, 0)

    acc_b[...] = jnp.zeros_like(acc_b)
    back[0] = jnp.broadcast_to(over_lanes(acc_a[...], features), (STEP, SEG, LANES))

    def centre(k, carry):
        v = conv[k] - back[0]
        conv[k] = v
        acc_b[...] += v * v
        return carry

    lax.fori_loop(0, slabs, centre, 0)
    back[1] = jnp.broadcast_to(lax.rsqrt(over_lanes(acc_b[...], features) + EPSILON), (STEP, SEG, LANES))
    acc_a[...] = jnp.zeros_like(acc_a)
    acc_b[...] = jnp.zeros_like(acc_b)

    def order_cot(j, carry):
        for k in range(slabs):
            deriv[k, j] = row(cots, k, j)
        return carry

    lax.fori_loop(0, STEP, order_cot, 0)
    small_rows = small.shape[0] // slabs // SEG * SEG

    def small_row(k, r):
        return pl.ds(pl.multiple_of(k * small_rows, SEG) + r, 1)

    def middle(k, carry):
        g = gain_mid_ref[:, pl.ds(pl.multiple_of(k * LANES, LANES), LANES)]
        hat = conv[k] * back[1]
        mixed = hat * g
        s = jax.nn.sigmoid(mixed)
        d = deriv[k] * keep[...] * (s * (1.0 + mixed * (1.0 - s)))
        dh = d * hat
        small[small_row(k, taps + 1), :] = jnp.sum(jnp.sum(dh, axis=0), axis=0, keepdims=True)
        conv[k] = hat
        d = d * g
        deriv[k] = d
        acc_a[...] += d
        acc_b[...] += dh * g
        return carry

    lax.fori_loop(0, slabs, middle, 0)
    acc_a[...] = jnp.broadcast_to(over_lanes(acc_a[...], features), (STEP, SEG, LANES))
    acc_b[...] = jnp.broadcast_to(over_lanes(acc_b[...], features), (STEP, SEG, LANES))

    def backward(k, carry):
        extend(ext_d, back[1] * (deriv[k] - acc_a[...] - conv[k] * acc_b[...]), taps)

        def put(j, v):
            deriv[k, j] = v * keep[j]

        tap_rows(ext_d, k, -1, put)
        half = taps // 2
        for t0 in (0, half):
            def one(b, totals):
                start = b * SEG
                ds = [ext_d[half + start + i] for i in range(SEG)]
                lines = [held[k, start + t0 + i] for i in range(half + SEG - 1)]
                return tuple(
                    functools.reduce(lambda p, q: p + q, [ds[i] * lines[i + t] for i in range(SEG)], totals[t])
                    for t in range(half)
                )

            totals = lax.fori_loop(0, STEP // SEG, one, tuple(jnp.zeros((SEG, LANES), f32) for _ in range(half)))
            for t in range(half):
                small[small_row(k, t0 + t), :] = jnp.sum(totals[t], axis=0, keepdims=True)
        d = deriv[k] * gate[k]
        lanes = pl.ds(pl.multiple_of(k * LANES, LANES), LANES)
        lanes_b = pl.ds(pl.multiple_of(features + k * LANES, LANES), LANES)
        grad[:, lanes] = d.reshape(tokens, LANES).astype(grad.dtype)
        db = d * left[k] * (1.0 - gate[k])
        grad[:, lanes_b] = db.reshape(tokens, LANES).astype(grad.dtype)
        return carry

    owner_rows = slots // (NX * 2)

    def half_cols(index, p):
        return pl.ds(pl.multiple_of(index * features + p * part_cols, part_cols), part_cols)

    def swap_part(p):
        return push(grad.at[:, half_cols(1 - c, p)], theirs_g.at[p], swap_send.at[1 + p], swap_recv.at[1 + p], sib)

    def make_terms(p):
        def one(ox, carry):
            rows = pl.ds(pl.multiple_of(ox * 2 * owner_rows, 64), 2 * owner_rows)
            term = jnp.dot(slots_t[rows, :], grad[:, half_cols(c, p)], preferred_element_type=f32)
            term = term + jnp.dot(theirs_t[rows, :], theirs_g[p], preferred_element_type=f32)
            for oy in range(2):
                for q in range(4):
                    for t in range(4):
                        first = (oy * 4 + q) * BLOCK
                        sums[p, ox, oy * 2 + t // 2, (t % 2) * 4 + q] = term[
                            first : first + BLOCK, t * LANES : (t + 1) * LANES
                        ].astype(sums.dtype)
            return carry

        lax.fori_loop(0, NX, one, 0)

    place_of = {"x": (x, NX, at_x), "y": (y, NY, at_y), "z": (z, NZ, at_z)}
    nears = {"x": near_x, "y": near_y, "z": near_z}
    direct_landing = ((mid_0, far_0), (mid_1, far_1), (mid_2, far_2))

    def part_flow(p):
        first, second, third_axis = PART_AXES[p]
        fixed = {}

        def chunk(axis, i, cut=None, half=None):
            index = []
            for a in ("x", "y", "z"):
                if a in fixed:
                    index.append(fixed[a])
                elif a == axis:
                    index.append(i % place_of[a][1])
                elif a == cut:
                    size = place_of[a][1] // 2
                    index.append(pl.ds(half * size, size))
                else:
                    index.append(slice(None))
            return sums.at[(p,) + tuple(index)]

        at, n, dev = place_of[first]
        rest = [a for a in ("x", "y", "z") if a != first]
        lead = tuple(place_of[a][1] for a in rest)
        half_size = lead[0] // 2
        hops = n // 2
        for step in range(hops):
            k = hops - step
            split = step == 0
            lines = []
            for w in (0, 1):
                sign = 1 if w == 0 else -1
                ref = nears[first].at[step, w]
                cut = (rest[0], w) if split else (None, None)
                if split:
                    ref = ref.at[pl.ds(w * half_size, half_size)]
                lines.append((sign, ref, cut, (send.at[p, step, w], recv.at[p, step, w])))
            for sign, ref, cut, sems in lines:
                push(chunk(first, at + n + sign * k, *cut), ref, *sems, dev(at + n + sign))
            yield
            for sign, ref, cut, sems in lines:
                landed(ref, *sems)
            if step < hops - 1:
                shape = (half_size,) + lead[1:] if split else lead
                for sign, ref, cut, sems in lines:
                    add_into(chunk(first, at + n + sign * (k - 1), *cut), [ref], shape)
            else:
                add_into(chunk(first, at), [ref for _, ref, _, _ in lines], lead)
        fixed[first] = at

        for stage, axis in enumerate((second, third_axis)):
            at, n, dev = place_of[axis]
            buffers = direct_landing[p][stage]
            for i in range(1, n):
                push(
                    chunk(axis, at + i), buffers.at[at],
                    direct_send.at[p, stage, i], direct_recv.at[p, stage, i], dev(at + i),
                )
            yield
            sources = [buffers.at[(at + n - i) % n] for i in range(1, n)]
            for i, ref in enumerate(sources):
                landed(ref, direct_send.at[p, stage, i + 1], direct_recv.at[p, stage, i + 1])
            add_into(chunk(axis, at), sources, (place_of[third_axis][1],) if stage == 0 else ())
            fixed[axis] = at

        finals[p, yl, z] = sums[p, x, y, z]
        for i in range(1, NZ):
            push(finals.at[p, yl, z], finals.at[p, yl, z], out_send.at[p, i], out_recv.at[p, i], at_z(z + i))
        yield
        for i in range(1, NZ):
            landed(finals.at[p, yl, (z + NZ - i) % NZ], out_send.at[p, i], out_recv.at[p, i])
        push(finals.at[p, yl], finals.at[p, yl], out_send.at[p, 0], out_recv.at[p, 0], to_ys)

        def pairs(layer, core, store):
            return [store.at[p, layer, pl.ds(zh * 4 + 2 * core, 2)] for zh in (0, 1)]

        def to_sibling(j, layer):
            for zh, (src, dst) in enumerate(zip(pairs(layer, 1 - c, finals), pairs(layer, 1 - c, other_finals))):
                push(src, dst, sib_send.at[p, j, zh], sib_recv.at[p, j, zh], sib)

        to_sibling(0, yl)
        yield
        landed(finals.at[p, 1 - yl], out_send.at[p, 0], out_recv.at[p, 0])
        to_sibling(1, 1 - yl)
        yield
        for j, layer in ((0, yl), (1, 1 - yl)):
            for zh, ref in enumerate(pairs(layer, c, other_finals)):
                landed(ref, sib_send.at[p, j, zh], sib_recv.at[p, j, zh])

    def small_flow():
        def spread(source, held_in, at, n, dev, first):
            for i in range(1, n):
                push(
                    source((at + i) % n), held_in.at[at],
                    small_send.at[first + i], small_recv.at[first + i], dev(at + i),
                )

        def collect(held_in, at, n, first):
            for i in range(1, n):
                landed(held_in.at[(at + n - i) % n], small_send.at[first + i], small_recv.at[first + i])

        def total_of(held_in, n):
            total = held_in[0]
            for i in range(1, n):
                total = total + held_in[i]
            return total

        for half in (0, 1):
            for k in range(NZ):
                small_split[half, k] = small[pl.ds((k * 2 + half) * SMALL, SMALL), :]
        push(small_split.at[1 - c], small_sib, small_send.at[8], small_recv.at[8], sib)
        yield
        landed(small_sib, small_send.at[8], small_recv.at[8])
        small_sum[...] = small_split[c] + small_sib[...]
        small_z[z] = small_sum[z]
        spread(lambda i: small_sum.at[i], small_z, z, NZ, at_z, 0)
        yield
        collect(small_z, z, NZ, 0)
        small_x[x] = total_of(small_z, NZ)
        spread(lambda i: small_x.at[x], small_x, x, NX, at_x, 8)
        yield
        collect(small_x, x, NX, 8)
        small_y[y] = total_of(small_x, NX)
        spread(lambda i: small_y.at[y], small_y, y, NY, at_y, 12)
        yield
        collect(small_y, y, NY, 12)
        small_out[c, z] = total_of(small_y, NY)
        spread(lambda i: small_out.at[c, z], small_out.at[c], z, NZ, at_z, 16)
        yield
        collect(small_out.at[c], z, NZ, 16)
        push(small_out.at[c], small_out.at[c], small_send.at[0], small_recv.at[0], sib)
        yield
        landed(small_out.at[1 - c], small_send.at[0], small_recv.at[0])

    flows = [part_flow(p) for p in range(PARTS)] + [small_flow()]
    over = [False] * len(flows)

    def resume(*which):
        for i in which:
            if not over[i]:
                try:
                    next(flows[i])
                except StopIteration:
                    over[i] = True

    part_slabs = slabs // PARTS

    def backward_some(p):
        lax.fori_loop(p * part_slabs, (p + 1) * part_slabs, backward, 0)

    def start_part(p):
        swap = swap_part(p)
        if p == 0:
            slots_copy.wait()
        swap.wait_recv()
        make_terms(p)
        resume(p)

    def slot_grads(i, carry):
        rows = weight[pl.ds(i * 2, 2)].reshape(2 * cap, width)
        g = contract_last(rows, grad[...])
        slots_t[pl.ds(pl.multiple_of(i * 2 * cap, 32), 2 * cap), :] = g.astype(slots_t.dtype)
        return carry

    def slot_some(lo, hi):
        lax.fori_loop(lo, hi, slot_grads, 0)

    def feature_grads(i, carry):
        owned = owner_ref[...]
        picked = jnp.concatenate([low[...] * slab_mask(owned, 2 * i + h) for h in (0, 1)], axis=0)
        g = jnp.transpose(jnp.dot(picked, slots_t[...], preferred_element_type=f32))
        for h in range(WIDE // LANES):
            deriv[i * (WIDE // LANES) + h] = g[:, h * LANES : (h + 1) * LANES].reshape(STEP, SEG, LANES)
        return carry

    def feature_some(lo, hi):
        lax.fori_loop(lo, hi, feature_grads, 0)

    def first_norm(j, totals):
        hats = [(row(natural, k, j) - means[j]) * inverses[j] for k in range(slabs)]
        gs = [deriv[k, j] for k in range(slabs)]
        totals = tuple(s + g * h for s, g, h in zip(totals, gs, hats))
        gs = [g * gain(gain_in_ref, k) for k, g in enumerate(gs)]
        total, cross = gs[0], gs[0] * hats[0]
        for g, h in zip(gs[1:], hats[1:]):
            total, cross = total + g, cross + g * h
        total, cross = over_lanes(total, features), over_lanes(cross, features)
        for k in range(slabs):
            v = row(cots, k, j) + inverses[j] * (gs[k] - total - hats[k] * cross)
            cots[k, pl.ds(j, SEG, stride=STEP), :] = v
        return totals

    backward_some(0)
    start_part(0)
    backward_some(1)
    start_part(1)
    resume(0)
    backward_some(2)
    start_part(2)
    resume(0)
    slot_some(0, 2)
    resume(1)
    slot_some(2, 4)
    resume(0, 2)
    slot_some(4, 8)
    resume(0)
    feature_some(0, 2)
    resume(1)
    feature_some(2, 4)
    resume(2, 0)
    feature_some(4, 6)
    resume(1)
    totals = tuple(jnp.zeros((SEG, LANES), f32) for _ in range(slabs))
    totals = lax.fori_loop(0, STEP // 2, first_norm, totals)
    resume(2, 0)
    totals = lax.fori_loop(STEP // 2, STEP, first_norm, totals)
    for k in range(slabs):
        small[pl.ds(k * small_rows + taps, 1), :] = jnp.sum(totals[k], axis=0, keepdims=True)
    resume(3, 1, 3, 2, 3, 0)
    for k in range(slabs):
        out_ref[:, pl.ds(k * LANES, LANES)] = cots[k].astype(out_ref.dtype)
    resume(3, 1, 2)
    while not all(over):
        resume(3, 0, 3, 1, 2)

    for layer in (0, 1):
        for zh in (0, 1):
            for p in range(PARTS):
                column = p * part_cols + (layer * 2 + zh) * LANES
                for source, which in ((finals, c), (other_finals, 1 - c)):
                    block = jnp.concatenate(
                        [wide(source[p, layer, zh * 4 + 2 * c + r]) for r in (0, 1)], axis=0
                    )
                    start = pl.multiple_of(which * features + column, LANES)
                    rows_ref[:, pl.ds(start, LANES)] = block.astype(rows_ref.dtype)
    for copy in pending:
        copy.wait_send()


def run_module(frames, cotangent, lengths, weight_slots, owner_rows, gain_in, gain_mid, taps):
    tokens, features = frames.shape
    cap, width = weight_slots.shape
    slots = owner_rows.shape[0]
    slabs = features // LANES
    count = taps.shape[0]
    bf, f32 = jnp.bfloat16, jnp.float32
    vmem = pl.BlockSpec(memory_space=pltpu.VMEM)
    slab = (slabs, STEP, SEG, LANES)
    plane = (STEP, SEG, LANES)
    block = (BLOCK, LANES)
    small = (SMALL, LANES)
    dma = pltpu.SemaphoreType.DMA
    return pl.pallas_call(
        module_kernel,
        out_shape=(
            jax.ShapeDtypeStruct((tokens, features), bf),
            jax.ShapeDtypeStruct((cap, width), bf),
            jax.ShapeDtypeStruct((2, NZ) + small, f32),
        ),
        in_specs=[pl.BlockSpec(memory_space=pltpu.SMEM)] + [vmem] * 7,
        out_specs=(vmem,) * 3,
        scratch_shapes=[
            pltpu.VMEM((slots // cap, cap, width), bf),
            pltpu.VMEM((slabs, tokens, LANES), f32),
            pltpu.VMEM((slabs, tokens, LANES), f32),
            pltpu.VMEM((tokens, features), bf),
            pltpu.VMEM((tokens, slots), bf),
            pltpu.VMEM((slots, tokens), bf),
            pltpu.VMEM((tokens, width), bf),
            pltpu.VMEM(plane, f32),
            pltpu.VMEM(plane, f32),
            pltpu.VMEM(slab, f32),
            pltpu.VMEM(slab, f32),
            pltpu.VMEM((slabs, STEP + count, SEG, LANES), f32),
            pltpu.VMEM(slab, f32),
            pltpu.VMEM(slab, f32),
            pltpu.VMEM((STEP + count, SEG, LANES), f32),
            pltpu.VMEM((slabs, count, SEG, LANES), f32),
            pltpu.VMEM(plane, f32),
            pltpu.VMEM(plane, f32),
            pltpu.VMEM(plane, f32),
            pltpu.VMEM((2,) + plane, f32),
            pltpu.VMEM((2 * NZ * SMALL, LANES), f32),
            pltpu.VMEM((2, NZ) + small, f32),
            pltpu.VMEM((slots, tokens), bf),
            pltpu.VMEM((PARTS, tokens, features // PARTS), bf),
            pltpu.VMEM((PARTS, NX, NY, NZ) + block, bf),
            pltpu.VMEM((LANES, slots), bf),
            pltpu.VMEM((2, 2, NY, NZ) + block, bf),
            pltpu.VMEM((2, 2, NX, NZ) + block, bf),
            pltpu.VMEM((4, 2, NX, NY) + block, bf),
            pltpu.VMEM((NX, NY) + block, bf),
            pltpu.VMEM((NY, NZ) + block, bf),
            pltpu.VMEM((NX, NZ) + block, bf),
            pltpu.VMEM((NY,) + block, bf),
            pltpu.VMEM((NZ,) + block, bf),
            pltpu.VMEM((NZ,) + block, bf),
            pltpu.VMEM((NZ,) + small, f32),
            pltpu.VMEM((NZ,) + small, f32),
            pltpu.VMEM((NZ,) + small, f32),
            pltpu.VMEM((NX,) + small, f32),
            pltpu.VMEM((NY,) + small, f32),
            pltpu.VMEM((PARTS, 2, NZ) + block, bf),
            pltpu.VMEM((PARTS, 2, NZ) + block, bf),
            dma,
            dma((53, PIECES)),
            dma((53, PIECES)),
            dma((1 + PARTS,)),
            dma((1 + PARTS,)),
            dma((PARTS, 4, 2)),
            dma((PARTS, 4, 2)),
            dma((PARTS, 2, NZ)),
            dma((PARTS, 2, NZ)),
            dma((24,)),
            dma((24,)),
            dma((PARTS, NZ)),
            dma((PARTS, NZ)),
            dma((PARTS, 2, 2)),
            dma((PARTS, 2, 2)),
        ],
        compiler_params=pltpu.CompilerParams(
            collective_id=0, has_side_effects=True, vmem_limit_bytes=63 << 20
        ),
        name="conv_module",
    )(lengths, frames, cotangent, weight_slots, owner_rows[None], gain_in[None], gain_mid[None], taps)


def per_device(frames, cotangent, lengths, weight_slots, owner_rows, gain_in, gain_mid, kernel):
    utterances, length, features = frames.shape
    taps = kernel.shape[0]
    slabs = features // LANES
    frame_grads, weight_grads, total = run_module(
        frames.reshape(length, features), cotangent.reshape(length, features), lengths, weight_slots,
        owner_rows, gain_in, gain_mid, kernel,
    )
    small_rows = 2 * NZ * SMALL
    each = small_rows // slabs // SEG * SEG
    total = total.transpose(1, 0, 2, 3).reshape(small_rows, LANES)[: slabs * each]
    total = total.reshape(slabs, each, LANES).transpose(1, 0, 2).reshape(each, features)
    return (frame_grads[None], weight_grads, total[taps], total[taps + 1], total[:taps])


def solution(mesh):
    in_specs = (
        P(("dp", "fsdp"), None, None),
        P(("dp", "fsdp"), None, None),
        P(("dp", "fsdp")),
        P("fsdp", None),
        P(),
        P(),
        P(),
        P(),
    )
    out_specs = (P(("dp", "fsdp"), None, None), P("fsdp", None), P(), P(), P())
    return jax.shard_map(
        per_device, mesh=mesh, in_specs=in_specs, out_specs=out_specs, check_vma=False
    )
```

profile of v0, /device:TPU:1, one launch (start us, length us, event | category | flops | bytes accessed | tf_op | source)
XLA Modules:
  0.0 168.5 jit_solution(2658550986855769331)
XLA Ops:
  1.3 0.0 copy-start.3
  1.3 0.0 copy-start.2
  1.3 1.3 broadcast_in_dim.13.gain_in_ref
  2.6 0.0 copy-done.3
  2.6 0.6 broadcast_in_dim.14.gain_mid_ref
  3.2 0.0 copy-done.2
  3.2 0.6 broadcast_in_dim.12.owner_ref
  3.8 159.9 %conv_module.1 = (bf16[256,1536]{1,0:T(8,128)(2,1)}, bf16[144,3072]{1,0:T(8,128)(2,1)}, f32[2,8,32,128]{3,2,1,0:T(8,128)}) custom-call(s32[1]{0:T(128)S(6)} %copy.19.length_ref, bf16[256,1536]{1,0:T(8,128)(2,1)} %bitcast.19, bf16[256,1536]{1,0:T(8,128)(2,1)} %bitcast.20, bf16[144,3072]{1,0:T(8,128)(2,1)} %w_ref.1, s32[1,2304]{1,0:T(1,128)} %broadcast_in_dim.12.owner_ref, ...), custom_call_target="tpu_custom_call" | custom-call | tf_op jit(solution)/shard_map/conv_module/pallas_call | solution.py:755
  163.8 0.0 copy-start.1
  163.8 1.0 copy.13
  164.8 0.6 slice_reduce_fusion
  165.5 0.7 copy_bitcast_fusion
  166.2 0.0 copy-start
  166.2 0.0 copy-done.1
  166.2 0.9 copy.20
  167.0 0.6 copy-done
  167.6 0.9 copy.21
  (1 shorter events, 0.0 us)
Async XLA Ops:
  1.3 1.3 copy-start.3
  1.3 1.9 %copy-start.2 = (s32[2304]{0:T(1024)S(1)}, s32[2304]{0:T(1024)}, u32[]{:S(2)}) copy-start(s32[2304]{0:T(1024)} %param.12) | copy-start | bytes 27652
  163.8 2.4 %copy-start.1 = (bf16[256,1536]{1,0:T(8,128)(2,1)S(1)}, bf16[256,1536]{1,0:T(8,128)(2,1)}, u32[]{:S(2)}) copy-start(bf16[256,1536]{1,0:T(8,128)(2,1)} %get-tuple-element.8) | copy-start | bytes 2359300
  166.2 1.5 copy-start
where the time goes:
time: 169 us
  Pallas kernels  160 us (95%)
  local copies, waits for them, and re-layouts  7.26 us (4%)
    pallas_call x1, Pallas kernels, run_module(): pl.pallas_call(module_kernel, out_shape=(jax.ShapeDtypeStruct((tokens, fe...  160 us

commit v1 on v0

--- a/solution.py
+++ b/solution.py
@@ -80,8 +80,9 @@
 
 
 def module_kernel(
-    length_ref, frames_ref, cot_ref, w_ref, owner_ref, gain_in_ref, gain_mid_ref, taps_ref,
-    out_ref, rows_ref, small_out,
+    length_ref, frames_hbm, cot_hbm, w_ref, owner_ref, gain_in_ref, gain_mid_ref, taps_ref,
+    out_ref, rows_ref, small_out, gin_out,
+    frames_ref, cot_ref, gin, gin_sib, gin_z, gin_x, gin_y, load_sem, gin_send, gin_recv,
     weight, natural, cots, normed, in_slots, slots_t, grad, means, inverses, left, gate, held,
     conv, deriv, ext_d, taps_wide, keep, acc_a, acc_b, back, small, small_split,
     theirs_t, theirs_g, sums, low, near_x, near_y, near_z, mid_0, mid_1, mid_2, far_0, far_1, far_2,
@@ -89,10 +90,14 @@
     keep_sem, w_send, w_recv, swap_send, swap_recv, send, recv, direct_send, direct_recv, small_send, small_recv,
     out_send, out_recv, sib_send, sib_recv,
 ):
+    load_frames = pltpu.make_async_copy(frames_hbm, frames_ref, load_sem.at[0])
+    load_cot = pltpu.make_async_copy(cot_hbm, cot_ref, load_sem.at[1])
+    load_frames.start()
+    load_cot.start()
     x, yh, yl, z, c = place()
     y = yh * 2 + yl
     f32 = jnp.float32
-    features = frames_ref.shape[1]
+    features = frames_hbm.shape[1]
     slabs = features // LANES
     taps = taps_ref.shape[0]
     slots = owner_ref.shape[1]
@@ -143,20 +148,23 @@
 
     xs = [x, (x + 3) % NX, (x + 1) % NX, (x + 2) % NX]
     to_xp, to_xm, to_zp, to_zm = at_x(x + 1), at_x(x + 3), at_z(z + 1), at_z(z + NZ - 1)
-    third = width // 3
+    span_x = width * 7 // 12
+    span_y = span_x // 2
+    rest_z = width - span_x
+    span_z = rest_z // 2
     piece_rows = cap // PIECES
     par = z % 2
-    base = par * third
+    base = par * rest_z
 
     def cols(start, size):
-        return pl.ds(pl.multiple_of(start, third // 2), size)
-
-    window = cols(base, 2 * third)
-    halves = [cols(base, third), cols(base + third, third)]
-    mine = cols(base + yl * third, third)
-    other = cols(base + (1 - yl) * third, third)
-    shared = [cols(base + par * third, third // 2), cols(base + par * third + third // 2, third // 2)]
-    theirs = [cols((1 - par) * 2 * third, third // 2), cols((1 - par) * 2 * third + third // 2, third // 2)]
+        return pl.ds(pl.multiple_of(start, LANES), size)
+
+    window = cols(base, span_x)
+    halves = [cols(base, span_y), cols(base + span_y, span_y)]
+    mine = cols(base + yl * span_y, span_y)
+    other = cols(base + (1 - yl) * span_y, span_y)
+    shared = [cols(par * span_x, span_z), cols(par * span_x + span_z, span_z)]
+    theirs = [cols((1 - par) * span_x, span_z), cols((1 - par) * span_x + span_z, span_z)]
 
     def owner(k, other_row):
         return (xs[k] * 2 + (1 - yh if other_row else yh)) * 2 + c
@@ -265,6 +273,7 @@
         return ref[:, pl.ds(k * LANES, LANES)]
 
     def prepare():
+        load_frames.wait()
         for k in range(slabs):
             lanes = pl.ds(k * LANES, LANES)
             natural[k] = wide(frames_ref[:, lanes])
@@ -274,6 +283,7 @@
         keep[...] = (seg_of * STEP + step_of < length_ref[0]).astype(f32)
 
     def prepare_cots():
+        load_cot.wait()
         for k in range(slabs):
             cots[k] = wide(cot_ref[:, pl.ds(k * LANES, LANES)])
         small[...] = jnp.zeros_like(small)
@@ -328,24 +338,25 @@
     fill = [part(norm_some, i) for i in range(STEP // 8)]
     fill += [part(choose, i) for i in range(slots // WIDE)] + [swap_slots, prepare_cots]
     steps = []
+    for q in range(PIECES):
+        if q + 1 < PIECES:
+            steps += [part(x_next, q + 1)]
+        steps += [part(x_near, 1, q), part(x_near, 2, q)]
+        if q == 0:
+            steps += [part(across, 0, r) for r in range(PIECES)]
+        else:
+            steps += [part(x_far, q - 1), part(across, 1, q - 1), part(across, 2, q - 1)]
+        if q == 1:
+            steps += [part(beside, 0, r) for r in range(PIECES)]
+        if q > 1:
+            steps += [part(across, 3, q - 2), part(beside, 1, q - 2), part(beside, 2, q - 2)]
     last = PIECES - 1
+    steps += [part(x_far, last), part(across, 1, last), part(across, 2, last)]
+    for q in range(last - 1, PIECES):
+        steps += [part(across, 3, q), part(beside, 1, q), part(beside, 2, q)]
     for q in range(PIECES):
-        if q < last:
-            steps += [part(x_next, q + 1)]
-        steps += [part(x_near, 1, q), part(x_near, 2, q), part(across, 0, q)]
-        if q > 0:
-            steps += [part(across, 1, q - 1), part(across, 2, q - 1), part(beside, 0, q - 1)]
-    steps += [part(beside, 0, last)]
-    steps += [part(x_far, 0), part(across, 1, last), part(across, 2, last)]
-    for q in range(PIECES):
-        steps += [part(beside, 1, q), part(beside, 2, q)]
-        if q < last:
-            steps += [part(x_far, q + 1)]
-        steps += [part(across, 3, q), part(z_in, 0, q), part(z_in, 1, q), part(z_in, 3, q)]
-    for q in range(PIECES):
-        steps += [part(beside, 3, q), part(z_in, 2, q), part(z_in, 4, q), part(z_in, 5, q)]
-    for q in range(PIECES):
-        steps += [part(z_in, 6, q)]
+        steps += [part(beside, 3, q)]
+    steps += [part(z_in, slot, q) for slot in (0, 1, 3, 2, 4, 5, 6) for q in range(PIECES)]
 
     prepare()
     for task in fill[:2]:
@@ -634,7 +645,25 @@
         yield
         landed(small_out.at[1 - c], small_send.at[0], small_recv.at[0])
 
-    flows = [part_flow(p) for p in range(PARTS)] + [small_flow()]
+    def gain_in_flow():
+        push(gin, gin_sib, gin_send.at[0, 0], gin_recv.at[0, 0], sib)
+        yield
+        landed(gin_sib, gin_send.at[0, 0], gin_recv.at[0, 0])
+        total = gin[...] + gin_sib[...]
+        for stage, (axis, store) in enumerate((("z", gin_z), ("x", gin_x), ("y", gin_y)), 1):
+            at, n, dev = place_of[axis]
+            store[at] = total
+            for i in range(1, n):
+                push(store.at[at], store.at[at], gin_send.at[stage, i], gin_recv.at[stage, i], dev(at + i))
+            yield
+            for i in range(1, n):
+                landed(store.at[(at + n - i) % n], gin_send.at[stage, i], gin_recv.at[stage, i])
+            total = store[0]
+            for i in range(1, n):
+                total = total + store[i]
+        gin_out[...] = total
+
+    flows = [part_flow(p) for p in range(PARTS)] + [small_flow(), gain_in_flow()]
     over = [False] * len(flows)
 
     def resume(*which):
@@ -692,6 +721,7 @@
             cots[k, pl.ds(j, SEG, stride=STEP), :] = v
         return totals
 
+    gin[...] = jnp.zeros_like(gin)
     backward_some(0)
     start_part(0)
     backward_some(1)
@@ -699,31 +729,31 @@
     resume(0)
     backward_some(2)
     start_part(2)
-    resume(0)
-    slot_some(0, 2)
+    resume(0, 3)
+    slot_some(0, 3)
+    resume(1, 3)
+    slot_some(3, 6)
+    resume(0, 2, 3)
+    slot_some(6, 8)
+    feature_some(0, 1)
+    resume(0, 3)
+    feature_some(1, 3)
     resume(1)
-    slot_some(2, 4)
-    resume(0, 2)
-    slot_some(4, 8)
-    resume(0)
-    feature_some(0, 2)
-    resume(1)
-    feature_some(2, 4)
-    resume(2, 0)
-    feature_some(4, 6)
-    resume(1)
+    feature_some(3, 5)
+    resume(2, 0, 3)
+    feature_some(5, 6)
     totals = tuple(jnp.zeros((SEG, LANES), f32) for _ in range(slabs))
     totals = lax.fori_loop(0, STEP // 2, first_norm, totals)
-    resume(2, 0)
+    resume(1, 3)
     totals = lax.fori_loop(STEP // 2, STEP, first_norm, totals)
     for k in range(slabs):
-        small[pl.ds(k * small_rows + taps, 1), :] = jnp.sum(totals[k], axis=0, keepdims=True)
-    resume(3, 1, 3, 2, 3, 0)
+        gin[pl.ds(k, 1), :] = jnp.sum(totals[k], axis=0, keepdims=True)
+    resume(4, 2, 0, 4, 1, 2, 4)
     for k in range(slabs):
         out_ref[:, pl.ds(k * LANES, LANES)] = cots[k].astype(out_ref.dtype)
-    resume(3, 1, 2)
+    resume(0, 4, 3)
     while not all(over):
-        resume(3, 0, 3, 1, 2)
+        resume(1, 2, 4, 0, 3)
 
     for layer in (0, 1):
         for zh in (0, 1):
@@ -751,6 +781,7 @@
     plane = (STEP, SEG, LANES)
     block = (BLOCK, LANES)
     small = (SMALL, LANES)
+    gin = (pl.cdiv(slabs, SEG) * SEG, LANES)
     dma = pltpu.SemaphoreType.DMA
     return pl.pallas_call(
         module_kernel,
@@ -758,10 +789,21 @@
             jax.ShapeDtypeStruct((tokens, features), bf),
             jax.ShapeDtypeStruct((cap, width), bf),
             jax.ShapeDtypeStruct((2, NZ) + small, f32),
+            jax.ShapeDtypeStruct(gin, f32),
         ),
-        in_specs=[pl.BlockSpec(memory_space=pltpu.SMEM)] + [vmem] * 7,
-        out_specs=(vmem,) * 3,
+        in_specs=[pl.BlockSpec(memory_space=pltpu.SMEM)] + [pl.BlockSpec(memory_space=pl.ANY)] * 3 + [vmem] * 4,
+        out_specs=(vmem,) * 4,
         scratch_shapes=[
+            pltpu.VMEM((tokens, features), bf),
+            pltpu.VMEM((tokens, features), bf),
+            pltpu.VMEM(gin, f32),
+            pltpu.VMEM(gin, f32),
+            pltpu.VMEM((NZ,) + gin, f32),
+            pltpu.VMEM((NX,) + gin, f32),
+            pltpu.VMEM((NY,) + gin, f32),
+            dma((2,)),
+            dma((4, NZ)),
+            dma((4, NZ)),
             pltpu.VMEM((slots // cap, cap, width), bf),
             pltpu.VMEM((slabs, tokens, LANES), f32),
             pltpu.VMEM((slabs, tokens, LANES), f32),
@@ -831,7 +873,7 @@
     utterances, length, features = frames.shape
     taps = kernel.shape[0]
     slabs = features // LANES
-    frame_grads, weight_grads, total = run_module(
+    frame_grads, weight_grads, total, gain_in_total = run_module(
         frames.reshape(length, features), cotangent.reshape(length, features), lengths, weight_slots,
         owner_rows, gain_in, gain_mid, kernel,
     )
@@ -839,7 +881,8 @@
     each = small_rows // slabs // SEG * SEG
     total = total.transpose(1, 0, 2, 3).reshape(small_rows, LANES)[: slabs * each]
     total = total.reshape(slabs, each, LANES).transpose(1, 0, 2).reshape(each, features)
-    return (frame_grads[None], weight_grads, total[taps], total[taps + 1], total[:taps])
+    gain_in_total = gain_in_total[:slabs].reshape(features)
+    return (frame_grads[None], weight_grads, gain_in_total, total[taps + 1], total[:taps])
 
 
 def solution(mesh):

time: 169 us -> 163 us (0.964)
  Pallas kernels: 160 us -> 153 us
    pallas_call x1, Pallas kernels: 160 us -> 153 us  [run_module(): pl.pallas_call(module_kernel, out_shape=(jax.ShapeDtypeStruct((tokens, fe...]
where the time goes in v1:
time: 163 us
  Pallas kernels  153 us (94%)
  local copies, waits for them, and re-layouts  8.54 us (5%)
    pallas_call x1, Pallas kernels, run_module(): pl.pallas_call(module_kernel, out_shape=(jax.ShapeDtypeStruct((tokens, fe...  153 us

profile of v1, /device:TPU:1, one launch (start us, length us, event | category | flops | bytes accessed | tf_op | source)
XLA Modules:
  0.0 163.0 jit_solution(11641716670254191566)
XLA Ops:
  1.3 0.0 copy-start.3
  1.3 0.0 copy-start.2
  1.3 1.3 broadcast_in_dim.13.gain_in_ref
  2.6 0.0 copy-done.3
  2.6 0.6 broadcast_in_dim.14.gain_mid_ref
  3.2 0.0 copy-done.2
  3.2 0.6 broadcast_in_dim.12.owner_ref
  3.8 153.1 %conv_module.1 = (bf16[256,1536]{1,0:T(8,128)(2,1)}, bf16[144,3072]{1,0:T(8,128)(2,1)}, f32[2,8,32,128]{3,2,1,0:T(8,128)}, f32[16,128]{1,0:T(8,128)}) custom-call(s32[1]{0:T(128)S(6)} %copy.19.length_ref, bf16[256,1536]{1,0:T(8,128)(2,1)} %bitcast.20, bf16[256,1536]{1,0:T(8,128)(2,1)} %bitcast.21, bf16[144,3072]{1,0:T(8,128)(2,1)} %w_ref.1, ...), custom_call_target="tpu_custom_call" | custom-call | tf_op jit(solution)/shard_map/conv_module/pallas_call | solution.py:786
  156.9 0.0 copy-start.1
  156.9 1.4 slice_bitcast_fusion.1
  158.3 1.0 copy.13
  159.3 0.6 slice_reduce_fusion
  159.9 0.7 copy_bitcast_fusion
  160.6 0.0 copy-start
  160.6 0.0 copy-done.1
  160.6 0.9 copy.20
  161.5 0.6 copy-done
  162.1 0.9 copy.21
  (1 shorter events, 0.0 us)
Async XLA Ops:
  1.3 1.3 copy-start.3
  1.3 1.9 %copy-start.2 = (s32[2304]{0:T(1024)S(1)}, s32[2304]{0:T(1024)}, u32[]{:S(2)}) copy-start(s32[2304]{0:T(1024)} %param.12) | copy-start | bytes 27652
  156.9 3.7 %copy-start.1 = (bf16[256,1536]{1,0:T(8,128)(2,1)S(1)}, bf16[256,1536]{1,0:T(8,128)(2,1)}, u32[]{:S(2)}) copy-start(bf16[256,1536]{1,0:T(8,128)(2,1)} %get-tuple-element.9) | copy-start | bytes 2359300
  160.6 1.5 copy-start

commit v2 on v1

--- a/solution.py
+++ b/solution.py
@@ -81,8 +81,8 @@
 
 def module_kernel(
     length_ref, frames_hbm, cot_hbm, w_ref, owner_ref, gain_in_ref, gain_mid_ref, taps_ref,
-    out_ref, rows_ref, small_out, gin_out,
-    frames_ref, cot_ref, gin, gin_sib, gin_z, gin_x, gin_y, load_sem, gin_send, gin_recv,
+    out_ref, rows_ref, taps_out, gains_out, gin_out,
+    small_out, frames_ref, cot_ref, gin, gin_sib, gin_z, gin_x, gin_y, load_sem, gin_send, gin_recv,
     weight, natural, cots, normed, in_slots, slots_t, grad, means, inverses, left, gate, held,
     conv, deriv, ext_d, taps_wide, keep, acc_a, acc_b, back, small, small_split,
     theirs_t, theirs_g, sums, low, near_x, near_y, near_z, mid_0, mid_1, mid_2, far_0, far_1, far_2,
@@ -100,7 +100,7 @@
     features = frames_hbm.shape[1]
     slabs = features // LANES
     taps = taps_ref.shape[0]
-    slots = owner_ref.shape[1]
+    slots = owner_ref.shape[0]
     blocks = features // WIDE
     tokens = STEP * SEG
     cap, width = w_ref.shape
@@ -270,7 +270,7 @@
         return ref[k, pl.ds(j, SEG, stride=STEP), :]
 
     def gain(ref, k):
-        return ref[:, pl.ds(k * LANES, LANES)]
+        return ref[pl.ds(k * LANES, LANES)].reshape(1, LANES)
 
     def prepare():
         load_frames.wait()
@@ -318,7 +318,7 @@
     def choose(i):
         span = pl.ds(i * WIDE, WIDE)
         rows = lax.broadcasted_iota(jnp.int32, (LANES, WIDE), 0)
-        owned = owner_ref[:, span]
+        owned = owner_ref[span].reshape(1, WIDE)
         line = jnp.where(rows == owned % LANES, 1.0, 0.0).astype(normed.dtype)
         low[:, span] = line
         picked = jnp.concatenate([line * slab_mask(owned, k) for k in range(slabs)], axis=0)
@@ -439,7 +439,7 @@
         return pl.ds(pl.multiple_of(k * small_rows, SEG) + r, 1)
 
     def middle(k, carry):
-        g = gain_mid_ref[:, pl.ds(pl.multiple_of(k * LANES, LANES), LANES)]
+        g = gain_mid_ref[pl.ds(pl.multiple_of(k * LANES, LANES), LANES)].reshape(1, LANES)
         hat = conv[k] * back[1]
         mixed = hat * g
         s = jax.nn.sigmoid(mixed)
@@ -697,7 +697,7 @@
         lax.fori_loop(lo, hi, slot_grads, 0)
 
     def feature_grads(i, carry):
-        owned = owner_ref[...]
+        owned = owner_ref[...].reshape(1, slots)
         picked = jnp.concatenate([low[...] * slab_mask(owned, 2 * i + h) for h in (0, 1)], axis=0)
         g = jnp.transpose(jnp.dot(picked, slots_t[...], preferred_element_type=f32))
         for h in range(WIDE // LANES):
@@ -765,6 +765,16 @@
                     )
                     start = pl.multiple_of(which * features + column, LANES)
                     rows_ref[:, pl.ds(start, LANES)] = block.astype(rows_ref.dtype)
+    for k in range(slabs):
+        lanes = pl.ds(k * LANES, LANES)
+        for m in range(small_rows // SEG):
+            group = (k * small_rows) // SEG + m
+            which, line = group // (SMALL // SEG), (group % (SMALL // SEG)) * SEG
+            value = small_out[which % 2, which // 2, pl.ds(line, SEG), :]
+            if m < taps // SEG:
+                taps_out[pl.ds(m * SEG, SEG), lanes] = value
+            else:
+                gains_out[:, lanes] = value
     for copy in pending:
         copy.wait_send()
 
@@ -788,12 +798,14 @@
         out_shape=(
             jax.ShapeDtypeStruct((tokens, features), bf),
             jax.ShapeDtypeStruct((cap, width), bf),
-            jax.ShapeDtypeStruct((2, NZ) + small, f32),
+            jax.ShapeDtypeStruct((count, features), f32),
+            jax.ShapeDtypeStruct((SEG, features), f32),
             jax.ShapeDtypeStruct(gin, f32),
         ),
         in_specs=[pl.BlockSpec(memory_space=pltpu.SMEM)] + [pl.BlockSpec(memory_space=pl.ANY)] * 3 + [vmem] * 4,
-        out_specs=(vmem,) * 4,
+        out_specs=(vmem,) * 5,
         scratch_shapes=[
+            pltpu.VMEM((2, NZ) + small, f32),
             pltpu.VMEM((tokens, features), bf),
             pltpu.VMEM((tokens, features), bf),
             pltpu.VMEM(gin, f32),
@@ -866,23 +878,18 @@
             collective_id=0, has_side_effects=True, vmem_limit_bytes=63 << 20
         ),
         name="conv_module",
-    )(lengths, frames, cotangent, weight_slots, owner_rows[None], gain_in[None], gain_mid[None], taps)
+    )(lengths, frames, cotangent, weight_slots, owner_rows, gain_in, gain_mid, taps)
 
 
 def per_device(frames, cotangent, lengths, weight_slots, owner_rows, gain_in, gain_mid, kernel):
     utterances, length, features = frames.shape
-    taps = kernel.shape[0]
     slabs = features // LANES
-    frame_grads, weight_grads, total, gain_in_total = run_module(
+    frame_grads, weight_grads, taps_total, gains_total, gain_in_total = run_module(
         frames.reshape(length, features), cotangent.reshape(length, features), lengths, weight_slots,
         owner_rows, gain_in, gain_mid, kernel,
     )
-    small_rows = 2 * NZ * SMALL
-    each = small_rows // slabs // SEG * SEG
-    total = total.transpose(1, 0, 2, 3).reshape(small_rows, LANES)[: slabs * each]
-    total = total.reshape(slabs, each, LANES).transpose(1, 0, 2).reshape(each, features)
     gain_in_total = gain_in_total[:slabs].reshape(features)
-    return (frame_grads[None], weight_grads, gain_in_total, total[taps + 1], total[:taps])
+    return (frame_grads[None], weight_grads, gain_in_total, gains_total[1], taps_total)
 
 
 def solution(mesh):

time: 163 us -> 161 us (0.988)
  local copies, waits for them, and re-layouts: 8.54 us -> 6.65 us
    broadcast_in_dim x3 -> x0, local copies, waits for them, and re-layouts: 2.51 us -> none  [the longest x1 1.31 us: run_module(): gain_in[None]]
    unnamed x10 -> x7, local copies, waits for them, and re-layouts: 2.37 us -> 3.86 us
where the time goes in v2:
time: 161 us
  Pallas kernels  153 us (95%)
  local copies, waits for them, and re-layouts  6.65 us (4%)
    pallas_call x1, Pallas kernels, run_module(): pl.pallas_call(module_kernel, out_shape=(jax.ShapeDtypeStruct((tokens, fe...  153 us
    unnamed x7, local copies, waits for them, and re-layouts  3.86 us

profile of v2, /device:TPU:1, one launch (start us, length us, event | category | flops | bytes accessed | tf_op | source)
XLA Modules:
  0.0 160.9 jit_solution(989478255336478732)
XLA Ops:
  1.3 152.9 %conv_module.1 = (bf16[256,1536]{1,0:T(8,128)(2,1)}, bf16[144,3072]{1,0:T(8,128)(2,1)}, f32[32,1536]{1,0:T(8,128)}, f32[8,1536]{1,0:T(8,128)}, f32[16,128]{1,0:T(8,128)}) custom-call(s32[1]{0:T(128)S(6)} %copy.16.length_ref, bf16[256,1536]{1,0:T(8,128)(2,1)} %bitcast.6, bf16[256,1536]{1,0:T(8,128)(2,1)} %bitcast.7, bf16[144,3072]{1,0:T(8,128)(2,1)} %w_ref.1, ...), custom_call_target="tpu_custom_call" | custom-call | tf_op jit(solution)/shard_map/conv_module/pallas_call | solution.py:796
  154.2 0.0 copy-start
  154.2 1.4 slice_bitcast_fusion
  155.6 1.4 slice_reduce_fusion
  157.0 2.1 %copy.17 = bf16[1,256,1536]{2,1,0:T(8,128)(2,1)} copy(bf16[1,256,1536]{2,1,0:T(8,128)(2,1)} %bitcast.5) | data formatting | bytes 1572864
  159.1 0.0 copy-done
  159.1 0.0 copy-start.1
  159.1 0.9 copy.18
  160.0 0.2 copy-done.1
  160.2 0.7 copy.19
Async XLA Ops:
  154.2 4.9 %copy-start = (bf16[144,3072]{1,0:T(8,128)(2,1)S(1)}, bf16[144,3072]{1,0:T(8,128)(2,1)}, u32[]{:S(2)}) copy-start(bf16[144,3072]{1,0:T(8,128)(2,1)} %get-tuple-element.21) | copy-start | bytes 2654212
  159.1 1.1 copy-start.1

commit v3 on v2

--- a/solution.py
+++ b/solution.py
@@ -81,7 +81,7 @@
 
 def module_kernel(
     length_ref, frames_hbm, cot_hbm, w_ref, owner_ref, gain_in_ref, gain_mid_ref, taps_ref,
-    out_ref, rows_ref, taps_out, gains_out, gin_out,
+    out_ref, rows_ref, taps_out, gain_mid_out, gain_in_out,
     small_out, frames_ref, cot_ref, gin, gin_sib, gin_z, gin_x, gin_y, load_sem, gin_send, gin_recv,
     weight, natural, cots, normed, in_slots, slots_t, grad, means, inverses, left, gate, held,
     conv, deriv, ext_d, taps_wide, keep, acc_a, acc_b, back, small, small_split,
@@ -661,7 +661,8 @@
             total = store[0]
             for i in range(1, n):
                 total = total + store[i]
-        gin_out[...] = total
+        for k in range(slabs):
+            gain_in_out[pl.ds(k * LANES, LANES)] = total[k]
 
     flows = [part_flow(p) for p in range(PARTS)] + [small_flow(), gain_in_flow()]
     over = [False] * len(flows)
@@ -774,7 +775,7 @@
             if m < taps // SEG:
                 taps_out[pl.ds(m * SEG, SEG), lanes] = value
             else:
-                gains_out[:, lanes] = value
+                gain_mid_out[lanes] = value[1]
     for copy in pending:
         copy.wait_send()
 
@@ -799,8 +800,8 @@
             jax.ShapeDtypeStruct((tokens, features), bf),
             jax.ShapeDtypeStruct((cap, width), bf),
             jax.ShapeDtypeStruct((count, features), f32),
-            jax.ShapeDtypeStruct((SEG, features), f32),
-            jax.ShapeDtypeStruct(gin, f32),
+            jax.ShapeDtypeStruct((features,), f32),
+            jax.ShapeDtypeStruct((features,), f32),
         ),
         in_specs=[pl.BlockSpec(memory_space=pltpu.SMEM)] + [pl.BlockSpec(memory_space=pl.ANY)] * 3 + [vmem] * 4,
         out_specs=(vmem,) * 5,
@@ -883,13 +884,11 @@
 
 def per_device(frames, cotangent, lengths, weight_slots, owner_rows, gain_in, gain_mid, kernel):
     utterances, length, features = frames.shape
-    slabs = features // LANES
-    frame_grads, weight_grads, taps_total, gains_total, gain_in_total = run_module(
+    frame_grads, weight_grads, taps_total, gain_mid_total, gain_in_total = run_module(
         frames.reshape(length, features), cotangent.reshape(length, features), lengths, weight_slots,
         owner_rows, gain_in, gain_mid, kernel,
     )
-    gain_in_total = gain_in_total[:slabs].reshape(features)
-    return (frame_grads[None], weight_grads, gain_in_total, gains_total[1], taps_total)
+    return (frame_grads[None], weight_grads, gain_in_total, gain_mid_total, taps_total)
 
 
 def solution(mesh):

time: 161 us -> 160 us (level)
  local copies, waits for them, and re-layouts: 6.65 us -> 5.04 us
    unnamed x7 -> x13, local copies, waits for them, and re-layouts: 3.86 us -> 5.04 us
where the time goes in v3:
time: 160 us; the launch traced here: 159 us
  Pallas kernels  153 us (96%)
  local copies, waits for them, and re-layouts  5.04 us (3%)
    pallas_call x1, Pallas kernels, run_module(): pl.pallas_call(module_kernel, out_shape=(jax.ShapeDtypeStruct((tokens, fe...  153 us
    unnamed x13, local copies, waits for them, and re-layouts  5.04 us

profile of v3, /device:TPU:1, one launch (start us, length us, event | category | flops | bytes accessed | tf_op | source)
XLA Modules:
  0.0 159.1 jit_solution(15301708985708272518)
XLA Ops:
  1.3 152.8 %conv_module.1 = (bf16[256,1536]{1,0:T(8,128)(2,1)}, bf16[144,3072]{1,0:T(8,128)(2,1)}, f32[32,1536]{1,0:T(8,128)}, f32[1536]{0:T(1024)}, f32[1536]{0:T(1024)}) custom-call(s32[1]{0:T(128)S(6)} %copy.18.length_ref, bf16[256,1536]{1,0:T(8,128)(2,1)} %bitcast.4, bf16[256,1536]{1,0:T(8,128)(2,1)} %bitcast.5, bf16[144,3072]{1,0:T(8,128)(2,1)} %w_ref.1, ...), custom_call_target="tpu_custom_call" | custom-call | tf_op jit(solution)/shard_map/conv_module/pallas_call | solution.py:797
  154.1 0.0 copy-start
  154.1 2.1 %copy.19 = bf16[1,256,1536]{2,1,0:T(8,128)(2,1)} copy(bf16[1,256,1536]{2,1,0:T(8,128)(2,1)} %bitcast.3) | data formatting | bytes 1572864
  156.2 0.0 copy-done
  156.2 0.0 copy-start.3
  156.2 0.0 copy-start.1
  156.2 0.9 copy.20
  157.2 0.0 copy-done.3
  157.2 0.0 copy-start.2
  157.2 0.6 copy.21
  157.8 0.1 copy-done.2
  157.9 0.6 copy.22
  158.5 0.0 copy-done.1
  158.5 0.7 copy.23
Async XLA Ops:
  154.1 2.2 %copy-start = (bf16[144,3072]{1,0:T(8,128)(2,1)S(1)}, bf16[144,3072]{1,0:T(8,128)(2,1)}, u32[]{:S(2)}) copy-start(bf16[144,3072]{1,0:T(8,128)(2,1)} %get-tuple-element.21) | copy-start | bytes 2654212
  156.2 0.9 copy-start.3
  156.2 2.2 %copy-start.1 = (f32[32,1536]{1,0:T(8,128)S(1)}, f32[32,1536]{1,0:T(8,128)}, u32[]{:S(2)}) copy-start(f32[32,1536]{1,0:T(8,128)} %get-tuple-element.24) | copy-start | bytes 589828
  157.2 0.7 copy-start.2
